TPU v7x, 32 devices: a whole 2x2x4 slice. The times are simulated.
32 devices in a mesh: dp: 8 (over z, core), fsdp: 4 (over y, x).
Axes of the slice: x: 2, y: 2, z: 4, core: 2. Of those that a mesh axis runs over, the one named last changes fastest.
Arguments:
- pixels: bfloat16 [32768, 768], P(('dp', 'fsdp')), may hold values from -6 to 6
- valid_mask: int32 [32768, 768], P(('dp', 'fsdp')), may hold values from 0 to 1
- size_groups: int32 [32], P(('dp', 'fsdp')), may hold values from 0 to 2
- code_index: int32 [4, 8192], P(None, ('dp', 'fsdp')), may hold values from 0 to 16383, as said below
- w_pixel: float32 [2, 768, 512], P(None, 'fsdp', 'dp'), may hold values from -0.625 to 0.625
- w_res: float32 [4, 4608, 512], P(None, 'fsdp', 'dp'), may hold values from -0.1875 to 0.1875
- w_scale: float32 [2, 2048, 512], P(None, 'fsdp', 'dp'), may hold values from -0.5 to 0.5
- w_latent: float32 [2, 512, 256], P(None, 'fsdp', 'dp'), may hold values from -0.75 to 0.75
- norm_gains: float32 [8, 512], replicated, may hold values from -0.9 to 1.5
- moment_pixel: float32 [2, 768, 512], P(None, 'fsdp', 'dp'), may hold values from -4.4703484e-08 to 4.4703484e-08
- moment_res: float32 [4, 4608, 512], P(None, 'fsdp', 'dp'), may hold values from -4.4703484e-08 to 4.4703484e-08
- moment_scale: float32 [2, 2048, 512], P(None, 'fsdp', 'dp'), may hold values from -4.4703484e-08 to 4.4703484e-08
- moment_latent: float32 [2, 512, 256], P(None, 'fsdp', 'dp'), may hold values from -4.4703484e-08 to 4.4703484e-08
- moment_gains: float32 [8, 512], replicated, may hold values from -1.4901161e-07 to 1.4901161e-07
- second_pixel: float32 [2, 768, 512], P(None, 'fsdp', 'dp'), may hold values from 7.84e-18 to 3.136e-17
- second_res: float32 [4, 4608, 512], P(None, 'fsdp', 'dp'), may hold values from 7.84e-18 to 3.136e-17
- second_scale: float32 [2, 2048, 512], P(None, 'fsdp', 'dp'), may hold values from 7.84e-18 to 3.136e-17
- second_latent: float32 [2, 512, 256], P(None, 'fsdp', 'dp'), may hold values from 7.84e-18 to 3.136e-17
- second_gains: float32 [8, 512], replicated, may hold values from 1e-16 to 4e-16
- ema_counts: float32 [16384], P(('dp', 'fsdp')), may hold values from 0.5 to 4
- ema_sums: float32 [16384, 256], P(('dp', 'fsdp')), may hold values from -6 to 6
Outputs:
- loss_parts: float32 [3], replicated
- grad_norm: float32 [1], replicated
- next_pixel: float32 [2, 768, 512], P(None, 'fsdp', 'dp')
- next_moment_pixel: float32 [2, 768, 512], P(None, 'fsdp', 'dp')
- next_second_pixel: float32 [2, 768, 512], P(None, 'fsdp', 'dp')
- copy_pixel: bfloat16 [2, 768, 512], P(None, 'fsdp', 'dp')
- next_res: float32 [4, 4608, 512], P(None, 'fsdp', 'dp')
- next_moment_res: float32 [4, 4608, 512], P(None, 'fsdp', 'dp')
- next_second_res: float32 [4, 4608, 512], P(None, 'fsdp', 'dp')
- copy_res: bfloat16 [4, 4608, 512], P(None, 'fsdp', 'dp')
- next_scale: float32 [2, 2048, 512], P(None, 'fsdp', 'dp')
- next_moment_scale: float32 [2, 2048, 512], P(None, 'fsdp', 'dp')
- next_second_scale: float32 [2, 2048, 512], P(None, 'fsdp', 'dp')
- copy_scale: bfloat16 [2, 2048, 512], P(None, 'fsdp', 'dp')
- next_latent: float32 [2, 512, 256], P(None, 'fsdp', 'dp')
- next_moment_latent: float32 [2, 512, 256], P(None, 'fsdp', 'dp')
- next_second_latent: float32 [2, 512, 256], P(None, 'fsdp', 'dp')
- copy_latent: bfloat16 [2, 512, 256], P(None, 'fsdp', 'dp')
- next_gains: float32 [8, 512], replicated
- next_moment_gains: float32 [8, 512], replicated
- next_second_gains: float32 [8, 512], replicated
- next_counts: float32 [16384], P(('dp', 'fsdp'))
- next_sums: float32 [16384, 256], P(('dp', 'fsdp'))
- codebook: float32 [16384, 256], P(('dp', 'fsdp'))
- codebook_copy: bfloat16 [16384, 256], P(('dp', 'fsdp'))
Inputs may be any that keep to these rules, and one draw needn't show every extreme that they name: `code_index`: among the 4 x 256 codes of one device's positions, at most 64 lie in any one device's block of 16384 / 32 consecutive codes, and on every device some block holds exactly 64 of them.
All inputs are finite; a program needn't handle non-finite values.
Results may differ from a plain program's by a relative error of at most 0.0061.
Values may be sent and summed in bfloat16 or wider, within the bound.
No kernel may reach another device: no remote copies, remote signals or barrier semaphores. Data moves between devices by JAX's collectives and lax.ppermute only.
A program may use at most 256 MiB of HBM per device.

v0:
```python
import jax
import jax.numpy as jnp
from jax import lax
from jax.sharding import PartitionSpec as P

C = 512
ZD = 256
K = 16384
GROUPS = 32
SIDE = 32
DEPTH = 4
STEP = 5
HIGH = lax.Precision.HIGHEST
TAPS = [(dy, dx) for dy in (-1, 0, 1) for dx in (-1, 0, 1)]
COMMIT_WEIGHT = 0.25
CLIP_AT = 1e-05
EMA_DECAY = 0.8
WEIGHT_RATE = 0.03
GAIN_RATE = 0.4


def geometry(groups, size, width):
    span = jnp.left_shift(jnp.ones_like(groups), groups)
    sides = size // 4 * span
    tile = jnp.arange(16, dtype=jnp.int32)[None, :]
    image = tile // 4 // span[:, None] * (4 // span[:, None]) + tile % 4 // span[:, None]
    member = (image[:, :, None] == jnp.arange(16, dtype=jnp.int32)[None, None, :]).astype(
        jnp.float32
    )
    count = (sides * sides).astype(jnp.float32) * (width // GROUPS)
    return (sides, member, count)


def image_means(field, member, count):
    batch, size, _, width = field.shape
    tile = size // 4
    sums = jnp.sum(field.reshape(batch, 4, tile, 4, tile, width), axis=(2, 4)).reshape(
        batch, 16, width
    )
    per_image = jnp.einsum("btm,btc->bmc", member, sums, precision=HIGH)
    grouped = (
        jnp.sum(per_image.reshape(batch, 16, GROUPS, width // GROUPS), axis=3)
        / count[:, None, None]
    )
    spread = jnp.einsum("btm,bmg->btg", member, grouped, precision=HIGH)
    full = jnp.repeat(spread, width // GROUPS, axis=2).reshape(batch, 4, 1, 4, 1, width)
    return jnp.broadcast_to(full, (batch, 4, tile, 4, tile, width)).reshape(
        batch, size, size, width
    )


def gn_silu(field, gamma, beta, geom):
    mean = image_means(field, geom[1], geom[2])
    centered = field - mean
    var = image_means(centered * centered, geom[1], geom[2])
    return jax.nn.silu(centered * lax.rsqrt(var + 1e-05) * gamma + beta)


def silu_slope(value):
    gate = jax.nn.sigmoid(value)
    return gate * (1.0 + value * (1.0 - gate))


def side_masks(sides, size, delta):
    pos = jnp.arange(size, dtype=jnp.int32)
    near = pos + delta
    inside = (near >= 0) & (near < size)
    same = near[None, :] // sides[:, None] == pos[None, :] // sides[:, None]
    return (inside[None, :] & same).astype(jnp.float32)


def shifted(act, sides, dy, dx):
    size = act.shape[1]
    padded = jnp.pad(act, ((0, 0), (1, 1), (1, 1), (0, 0)))
    part = padded[:, 1 + dy : 1 + dy + size, 1 + dx : 1 + dx + size, :]
    keep = side_masks(sides, size, dy)[:, :, None] * side_masks(sides, size, dx)[:, None, :]
    return part * keep[..., None].astype(act.dtype)


def along_rows(left, right):
    return lax.dot_general(
        left, right, (((0,), (0,)), ((), ())), preferred_element_type=jnp.float32
    )


def along_cols(left, right):
    return lax.dot_general(
        left, right, (((1,), (1,)), ((), ())), preferred_element_type=jnp.float32
    )


def conv_forward(act, taps, geom):
    width = act.shape[3]
    total = jnp.zeros((act.shape[0] * act.shape[1] * act.shape[2], width), jnp.float32)
    for index, (dy, dx) in enumerate(TAPS):
        piece = shifted(act, geom[0], dy, dx).reshape(-1, width)
        total = total + jnp.dot(piece, taps[index], preferred_element_type=jnp.float32)
    return total.reshape(act.shape)


def conv_backward(act, taps, grad_out, geom):
    width = act.shape[3]
    grad_low = grad_out.reshape(-1, width).astype(jnp.bfloat16)
    weight_parts = []
    grad_act = jnp.zeros(act.shape, jnp.float32)
    for index, (dy, dx) in enumerate(TAPS):
        piece = shifted(act, geom[0], dy, dx).reshape(-1, width)
        weight_parts.append(along_rows(piece, grad_low))
        back = along_cols(grad_low, taps[index]).reshape(act.shape)
        grad_act = grad_act + shifted(back, geom[0], -dy, -dx)
    return (jnp.concatenate(weight_parts, axis=0), grad_act)


def block_forward(field, taps_pair, gains, first, geom):
    a_one = gn_silu(field, gains[first], gains[4 + first], geom).astype(jnp.bfloat16)
    t_one = conv_forward(a_one, taps_pair[0], geom)
    a_two = gn_silu(t_one, gains[first + 1], gains[5 + first], geom).astype(jnp.bfloat16)
    t_two = conv_forward(a_two, taps_pair[1], geom)
    return (field + t_two, (field, a_one, t_one, a_two))


def block_backward(grad, kept, taps_pair, gains, first, geom):
    field, a_one, t_one, a_two = kept
    grad_two, d_a_two = conv_backward(a_two, taps_pair[1], grad, geom)
    _, pull = jax.vjp(
        lambda x, g, b: gn_silu(x, g, b, geom), t_one, gains[first + 1], gains[5 + first]
    )
    d_t_one, scale_two, shift_two = pull(d_a_two)
    grad_one, d_a_one = conv_backward(a_one, taps_pair[0], d_t_one, geom)
    _, pull = jax.vjp(lambda x, g, b: gn_silu(x, g, b, geom), field, gains[first], gains[4 + first])
    d_field, scale_one, shift_one = pull(d_a_one)
    return (grad + d_field, (grad_one, grad_two), (scale_one, scale_two, shift_one, shift_two))


def to_depth(field):
    batch, size, _, width = field.shape
    half = size // 2
    parts = field.reshape(batch, half, 2, half, 2, width).transpose(0, 1, 3, 2, 4, 5)
    return parts.reshape(batch * half * half, 4 * width)


def from_depth(rows, batch, size):
    half = size // 2
    width = rows.shape[1] // 4
    parts = rows.reshape(batch, half, half, 2, 2, width).transpose(0, 1, 3, 2, 4, 5)
    return parts.reshape(batch, size, size, width)


def fetch(shard):
    cols = lax.all_gather(shard.astype(jnp.bfloat16), "dp", axis=1, tiled=True)
    return lax.all_gather(cols, "fsdp", axis=0, tiled=True)


def backward_copy(shard, ready):
    return fetch(shard).reshape(ready.shape)


def reduce_grad(full):
    rows = lax.psum_scatter(full, "fsdp", scatter_dimension=0, tiled=True)
    return lax.psum_scatter(rows, "dp", scatter_dimension=1, tiled=True)


def adam_step(weight, moment, second, grad, rate):
    moment_new = 0.5 * moment + 0.5 * grad
    second_new = 0.5 * second + 0.5 * grad * grad
    fix = 1.0 - 0.5**STEP
    weight_new = weight - rate * (
        moment_new / fix / (jnp.sqrt(second_new / fix) + 1e-12) + 0.01 * weight
    )
    return (weight_new, moment_new, second_new)


def owner_slots(flat_codes, devices, capacity, rows_own):
    owner = flat_codes // rows_own
    order = jnp.argsort(owner, stable=True)
    ranked = owner[order]
    first = jnp.searchsorted(ranked, jnp.arange(devices, dtype=jnp.int32))
    place = jnp.arange(flat_codes.shape[0], dtype=jnp.int32) - first[ranked]
    return jnp.zeros_like(flat_codes).at[order].set(ranked * capacity + place)


def on_device(
    pixels,
    valid_mask,
    size_groups,
    code_index,
    w_pixel,
    w_res,
    w_scale,
    w_latent,
    norm_gains,
    moment_pixel,
    moment_res,
    moment_scale,
    moment_latent,
    moment_gains,
    second_pixel,
    second_res,
    second_scale,
    second_latent,
    second_gains,
    ema_counts,
    ema_sums,
):
    canv = size_groups.shape[0]
    n_outer = lax.axis_size("dp")
    n_inner = lax.axis_size("fsdp")
    devices = n_outer * n_inner
    latent_all = code_index.shape[1] * devices
    rows = ema_sums.shape[0]
    flat_codes = code_index.reshape(-1)
    capacity = max(2, 2 * flat_codes.shape[0] // devices)
    slot = owner_slots(flat_codes, devices, capacity, rows)
    local_row = flat_codes % rows
    geom = geometry(size_groups, SIDE, C)
    mask = valid_mask.astype(jnp.float32)
    total_valid = lax.psum(jnp.sum(mask), ("dp", "fsdp"))
    book = (ema_sums / ema_counts[:, None]).astype(jnp.bfloat16)
    wanted = jnp.full((devices * capacity,), -1, jnp.int32).at[slot].set(local_row)
    wanted = wanted.reshape(n_outer, n_inner, capacity)
    asked = lax.all_to_all(
        lax.all_to_all(wanted, "dp", split_axis=0, concat_axis=0, tiled=True),
        "fsdp",
        split_axis=1,
        concat_axis=1,
        tiled=True,
    )
    answer = jnp.take(book, jnp.maximum(asked, 0), axis=0)
    replies = lax.all_to_all(
        lax.all_to_all(answer, "dp", split_axis=0, concat_axis=0, tiled=True),
        "fsdp",
        split_axis=1,
        concat_axis=1,
        tiled=True,
    )
    picked_rows = replies.reshape(devices * capacity, -1)[slot].reshape(
        code_index.shape + (book.shape[1],)
    )
    q_cum = jnp.cumsum(picked_rows.astype(jnp.float32), axis=0)
    patch_in = fetch(w_pixel[0])
    field = jnp.dot(pixels, patch_in, preferred_element_type=jnp.float32).reshape(
        canv, SIDE, SIDE, C
    )
    enc_taps = (fetch(w_res[0]).reshape(9, C, C), fetch(w_res[1]).reshape(9, C, C))
    field, kept_enc = block_forward(field, enc_taps, norm_gains, 0, geom)
    e_four = to_depth(field.astype(jnp.bfloat16))
    w_down = fetch(w_scale[0])
    hidden = jnp.dot(e_four, w_down, preferred_element_type=jnp.float32)
    s_one = jax.nn.silu(hidden).astype(jnp.bfloat16)
    w_proj = fetch(w_latent[0])
    latent = jnp.dot(s_one, w_proj, preferred_element_type=jnp.float32)
    diff = latent[None] - q_cum
    commit = jnp.sum(diff * diff)
    shift = q_cum[DEPTH - 1] - latent
    quant = (latent + shift).astype(jnp.bfloat16)
    w_back = fetch(w_latent[1])
    inner = along_cols(quant, w_back)
    s_two = jax.nn.silu(inner).astype(jnp.bfloat16)
    w_up = fetch(w_scale[1])
    upper = along_cols(s_two, w_up)
    dec_field = from_depth(upper, canv, SIDE)
    dec_taps = (fetch(w_res[2]).reshape(9, C, C), fetch(w_res[3]).reshape(9, C, C))
    dec_field, kept_dec = block_forward(dec_field, dec_taps, norm_gains, 2, geom)
    outer = jax.nn.silu(dec_field).astype(jnp.bfloat16).reshape(-1, C)
    w_head = fetch(w_pixel[1])
    recon = along_cols(outer, w_head)
    err = recon - pixels.astype(jnp.float32)
    smooth = jnp.sqrt(err * err + 1.0)
    l1_local = jnp.sum(mask * (smooth - 1.0))
    grad_rec = (mask * err / smooth / total_valid).astype(jnp.bfloat16)
    d_head = along_rows(grad_rec, outer)
    head_b = backward_copy(w_pixel[1], w_head)
    d_outer = jnp.dot(grad_rec, head_b, preferred_element_type=jnp.float32)
    d_dec = (d_outer * silu_slope(dec_field.reshape(-1, C))).reshape(dec_field.shape)
    dec_b = (backward_copy(w_res[2], dec_taps[0]), backward_copy(w_res[3], dec_taps[1]))
    d_dec, dec_grads, dec_gain = block_backward(d_dec, kept_dec, dec_b, norm_gains, 2, geom)
    d_upper = to_depth(d_dec).astype(jnp.bfloat16)
    d_up = along_rows(d_upper, s_two)
    up_b = backward_copy(w_scale[1], w_up)
    d_s_two = jnp.dot(d_upper, up_b, preferred_element_type=jnp.float32)
    d_inner = (d_s_two * silu_slope(inner)).astype(jnp.bfloat16)
    d_back = along_rows(d_inner, quant)
    back_b = backward_copy(w_latent[1], w_back)
    d_quant = jnp.dot(d_inner, back_b, preferred_element_type=jnp.float32)
    d_latent = d_quant + 2.0 * COMMIT_WEIGHT / (latent_all * ZD) * jnp.sum(diff, axis=0)
    d_latent = d_latent.astype(jnp.bfloat16)
    d_proj = along_rows(s_one, d_latent)
    proj_b = backward_copy(w_latent[0], w_proj)
    d_s_one = along_cols(d_latent, proj_b)
    d_hidden = (d_s_one * silu_slope(hidden)).astype(jnp.bfloat16)
    d_down = along_rows(e_four, d_hidden)
    down_b = backward_copy(w_scale[0], w_down)
    d_e_four = along_cols(d_hidden, down_b)
    d_enc = from_depth(d_e_four, canv, SIDE)
    enc_b = (backward_copy(w_res[0], enc_taps[0]), backward_copy(w_res[1], enc_taps[1]))
    d_enc, enc_grads, enc_gain = block_backward(d_enc, kept_enc, enc_b, norm_gains, 0, geom)
    d_first = d_enc.reshape(-1, C).astype(jnp.bfloat16)
    d_patch = along_rows(pixels, d_first)
    grad_pixel = jnp.stack([reduce_grad(d_patch), reduce_grad(d_head)])
    grad_res = jnp.stack(
        [
            reduce_grad(enc_grads[0]),
            reduce_grad(enc_grads[1]),
            reduce_grad(dec_grads[0]),
            reduce_grad(dec_grads[1]),
        ]
    )
    grad_scale = jnp.stack([reduce_grad(d_down), reduce_grad(d_up)])
    grad_latent = jnp.stack([reduce_grad(d_proj), reduce_grad(d_back)])
    gain_local = jnp.stack(
        [
            enc_gain[0],
            enc_gain[1],
            dec_gain[0],
            dec_gain[1],
            enc_gain[2],
            enc_gain[3],
            dec_gain[2],
            dec_gain[3],
        ]
    )
    grad_gains, smooth_sum, commit_sum = lax.psum((gain_local, l1_local, commit), ("dp", "fsdp"))
    shard_squares = jnp.sum(grad_pixel * grad_pixel) + jnp.sum(grad_res * grad_res)
    shard_squares = (
        shard_squares + jnp.sum(grad_scale * grad_scale) + jnp.sum(grad_latent * grad_latent)
    )
    total_squares = lax.psum(shard_squares, ("dp", "fsdp")) + jnp.sum(grad_gains * grad_gains)
    norm = jnp.sqrt(total_squares)
    factor = CLIP_AT / jnp.maximum(norm, CLIP_AT)
    groups_all = [
        (w_pixel, moment_pixel, second_pixel, grad_pixel),
        (w_res, moment_res, second_res, grad_res),
        (w_scale, moment_scale, second_scale, grad_scale),
        (w_latent, moment_latent, second_latent, grad_latent),
    ]
    outputs = [jnp.stack([smooth_sum, total_valid, commit_sum]), norm.reshape(1)]
    for weight, moment, second, grad in groups_all:
        weight_new, moment_new, second_new = adam_step(
            weight, moment, second, grad * factor, WEIGHT_RATE
        )
        outputs += [weight_new, moment_new, second_new, weight_new.astype(jnp.bfloat16)]
    outputs += list(
        adam_step(norm_gains, moment_gains, second_gains, grad_gains * factor, GAIN_RATE)
    )
    prev = jnp.concatenate([jnp.zeros_like(q_cum[:1]), q_cum[:-1]], axis=0)
    resid = (latent[None] - prev).astype(jnp.bfloat16).reshape(-1, ZD)
    block_len = min(K, 2048)

    def code_block(start):
        onehot = (
            flat_codes[:, None] == start + jnp.arange(block_len, dtype=jnp.int32)[None, :]
        ).astype(jnp.bfloat16)
        return (along_rows(onehot, resid), jnp.sum(onehot, axis=0, dtype=jnp.float32))

    sums_all, counts_all = lax.map(code_block, jnp.arange(0, K, block_len, dtype=jnp.int32))
    sums_all = sums_all.reshape(K, ZD)
    counts_all = counts_all.reshape(K)
    sums_total, counts_total = lax.psum((sums_all, counts_all), ("dp", "fsdp"))
    start_row = lax.axis_index(("dp", "fsdp")) * rows
    my_sums = lax.dynamic_slice_in_dim(sums_total, start_row, rows, 0)
    my_counts = lax.dynamic_slice_in_dim(counts_total, start_row, rows, 0)
    counts_new = EMA_DECAY * ema_counts + (1.0 - EMA_DECAY) * my_counts
    sums_new = EMA_DECAY * ema_sums + (1.0 - EMA_DECAY) * my_sums
    book_new = sums_new / counts_new[:, None]
    outputs += [counts_new, sums_new, book_new, book_new.astype(jnp.bfloat16)]
    return tuple(outputs)


def solution(mesh):
    placed = (
        P(("dp", "fsdp"), None),
        P(("dp", "fsdp"), None),
        P(("dp", "fsdp")),
        P(None, ("dp", "fsdp")),
        P(None, "fsdp", "dp"),
        P(None, "fsdp", "dp"),
        P(None, "fsdp", "dp"),
        P(None, "fsdp", "dp"),
        P(),
        P(None, "fsdp", "dp"),
        P(None, "fsdp", "dp"),
        P(None, "fsdp", "dp"),
        P(None, "fsdp", "dp"),
        P(),
        P(None, "fsdp", "dp"),
        P(None, "fsdp", "dp"),
        P(None, "fsdp", "dp"),
        P(None, "fsdp", "dp"),
        P(),
        P(("dp", "fsdp")),
        P(("dp", "fsdp"), None),
    )
    return jax.shard_map(
        on_device,
        mesh=mesh,
        in_specs=placed,
        out_specs=(
            P(),
            P(),
            P(None, "fsdp", "dp"),
            P(None, "fsdp", "dp"),
            P(None, "fsdp", "dp"),
            P(None, "fsdp", "dp"),
            P(None, "fsdp", "dp"),
            P(None, "fsdp", "dp"),
            P(None, "fsdp", "dp"),
            P(None, "fsdp", "dp"),
            P(None, "fsdp", "dp"),
            P(None, "fsdp", "dp"),
            P(None, "fsdp", "dp"),
            P(None, "fsdp", "dp"),
            P(None, "fsdp", "dp"),
            P(None, "fsdp", "dp"),
            P(None, "fsdp", "dp"),
            P(None, "fsdp", "dp"),
            P(),
            P(),
            P(),
            P(("dp", "fsdp")),
            P(("dp", "fsdp"), None),
            P(("dp", "fsdp"), None),
            P(("dp", "fsdp"), None),
        ),
        check_vma=False,
    )
```

profile of v0, /device:TPU:12, one launch (start us, length us, event | category | flops | bytes accessed | tf_op | source)
XLA Modules:
  0.0 1944.9 jit_solution(17899605121491176382)
XLA Ops:
  11.5 22.5 %all-gather.31.cloned.1.call-done = bf16[1,1152,512]{1,2,0:T(8,128)(2,1)} async-done(((bf16[1,1152,64]{1,2,0:T(8,128)(2,1)}), bf16[1,1152,512]{1,2,0:T(8,128)(2,1)}) %all-gather.31.cloned.1.call-update) | async-done | bytes 1179664 | tf_op jit(solution)/shard_map/all_gather | solution.py:150
  36.5 22.2 %all-gather.35.cloned.1.call-done = bf16[1,1152,512]{1,2,0:T(8,128)(2,1)} async-done(((bf16[1,1152,64]{1,2,0:T(8,128)(2,1)}), bf16[1,1152,512]{1,2,0:T(8,128)(2,1)}) %all-gather.35.cloned.1.call-update) | async-done | bytes 1179664 | tf_op jit(solution)/shard_map/all_gather | solution.py:150
  61.2 15.9 all-gather.6
  77.2 16.3 all-gather.12
  105.0 8.0 while.37
  119.3 15.9 fusion.437
  145.1 5.2 all-to-all-start
  151.1 14.2 all-gather
  165.4 12.4 all-gather.1
  192.5 7.5 gather_fusion.2
  201.3 5.3 all-to-all-start.2
  208.5 29.5 %all-gather.10 = bf16[1,128,256]{1,2,0:T(8,128)(2,1)S(1)} all-gather(bf16[1,128,32]{1,2,0:T(8,128)(2,1)S(1)} %get-tuple-element.455), channel_id=12, replica_groups=mesh['dp'=8,'fsdp'=4] {'dp'}, dimensions={2}, use_global_device_ids=true | all-gather | bytes 73728 | tf_op jit(solution)/shard_map/all_gather | solution.py:150
  238.0 14.3 all-gather.18
  260.5 5.7 all-to-all-start.3
  266.2 15.3 all-gather.8
  287.8 11.7 all-gather.9
  299.5 8.7 all-gather.11
  308.2 12.0 all-gather.19
  320.2 5.5 fusion.150
  327.4 5.0 gather_fusion.3
  364.2 5.3 fusion.158
  419.4 5.1 fusion.166
  445.5 5.4 fusion.174
  464.8 6.6 multiply_reduce_fusion
  471.4 41.4 %psum.50 = f32[]{:T(128)} all-reduce(f32[]{:T(128)} %get-tuple-element.298), channel_id=1, replica_groups=mesh['dp'=8,'fsdp'=4] {'dp','fsdp'}, use_global_device_ids=true, to_apply=%region_27.30 | all-reduce | flops 1 | bytes 8 | tf_op jit(solution)/shard_map/psum | solution.py:217
  512.8 6.2 divide_convert_fusion
  565.6 9.8 fusion.495
  579.8 5.7 fusion.511
  627.8 8.0 fusion.496
  641.4 5.3 fusion.510
  671.8 8.6 fusion.497
  795.2 49.7 %while.36 = (s32[]{:T(128)}, f32[8,2048,256]{2,1,0:T(8,128)}, f32[8,2048]{1,0:T(8,128)S(1)}, s32[4,256]{1,0:T(4,128)S(1)}, s32[8]{0:T(128)S(1)}, /*index=5*/bf16[1024,256]{1,0:T(8,128)(2,1)S(1)}, s32[]{:T(128)}, s32[]{:T(128)}) while((s32[]{:T(128)}, f32[8,2048,256]{2,1,0:T(8,128)}, f32[8,2048]{1,0:T(8,128)S(1)}, s32[4,256]{1,0:T(4,128)S(1)}, ...), condition=%wide.region_84.87_spmd, body=%wide.region_82.86_spmd.sunk | while | flops 1084227584 | bytes 2687093 | solution.py:355
  851.7 95.4 %reduce-scatter.45.cloned.1.call-done = f32[1152,512]{1,0:T(8,128)} async-done(((f32[4608,512]{1,0:T(8,128)}), f32[1152,512]{1,0:T(8,128)}) %reduce-scatter.45.cloned.1.call-update) | async-done | bytes 2359312 | tf_op jit(solution)/shard_map/reduce_scatter | solution.py:159
  950.2 94.9 %reduce-scatter.47.cloned.1.call-done = f32[1152,512]{1,0:T(8,128)} async-done(((f32[4608,512]{1,0:T(8,128)}), f32[1152,512]{1,0:T(8,128)}) %reduce-scatter.47.cloned.1.call-update) | async-done | bytes 2359312 | tf_op jit(solution)/shard_map/reduce_scatter | solution.py:159
  1048.3 95.0 %reduce-scatter.49.cloned.1.call-done = f32[1152,512]{1,0:T(8,128)} async-done(((f32[4608,512]{1,0:T(8,128)}), f32[1152,512]{1,0:T(8,128)}) %reduce-scatter.49.cloned.1.call-update) | async-done | bytes 2359312 | tf_op jit(solution)/shard_map/reduce_scatter | solution.py:159
  1146.4 94.9 %reduce-scatter.51.cloned.1.call-done = f32[1152,512]{1,0:T(8,128)} async-done(((f32[4608,512]{1,0:T(8,128)}), f32[1152,512]{1,0:T(8,128)}) %reduce-scatter.51.cloned.1.call-update) | async-done | bytes 2359312 | tf_op jit(solution)/shard_map/reduce_scatter | solution.py:159
  1245.8 25.0 %reduce-scatter.77.cloned.1.call-done = f32[32,128]{1,0:T(8,128)} async-done(((f32[256,128]{1,0:T(8,128)}), f32[32,128]{1,0:T(8,128)}) %reduce-scatter.77.cloned.1.call-update) | async-done | bytes 16400
  1271.7 30.3 %reduce-scatter.79.cloned.1.call-done = f32[32,128]{1,0:T(8,128)} async-done(((f32[256,128]{1,0:T(8,128)}), f32[32,128]{1,0:T(8,128)}) %reduce-scatter.79.cloned.1.call-update) | async-done | bytes 16400
  1303.5 30.4 %reduce-scatter.43.cloned.1.call-done = f32[192,64]{0,1:T(8,128)} async-done(((f32[192,512]{0,1:T(8,128)}), f32[192,64]{0,1:T(8,128)}) %reduce-scatter.43.cloned.1.call-update) | async-done | bytes 49168 | tf_op jit(solution)/shard_map/reduce_scatter | solution.py:160
  1334.0 31.9 %reduce-scatter.41.cloned.1.call-done = f32[192,64]{0,1:T(8,128)} async-done(((f32[192,512]{0,1:T(8,128)}), f32[192,64]{0,1:T(8,128)}) %reduce-scatter.41.cloned.1.call-update) | async-done | bytes 49168 | tf_op jit(solution)/shard_map/reduce_scatter | solution.py:160
  1367.4 288.5 %all-reduce.41.cloned.1.call-done = (f32[16384]{0:T(1024)}, f32[16384,256]{1,0:T(8,128)}) async-done(((f32[16384]{0:T(1024)}, f32[16384,256]{1,0:T(8,128)}), (f32[16384]{0:T(1024)}, f32[16384,256]{1,0:T(8,128)})) %all-reduce.41.cloned.1.call-update) | async-done | bytes 16842768 | tf_op jit(solution)/shard_map/psum | solution.py:358
  1658.8 28.4 %reduce-scatter.75.cloned.1.call-done = f32[64,512]{1,0:T(8,128)} async-done(((f32[512,512]{1,0:T(8,128)}), f32[64,512]{1,0:T(8,128)}) %reduce-scatter.75.cloned.1.call-update) | async-done | bytes 131088
  1687.2 33.6 %reduce-scatter.73.cloned.1.call-done = f32[64,512]{1,0:T(8,128)} async-done(((f32[512,512]{1,0:T(8,128)}), f32[64,512]{1,0:T(8,128)}) %reduce-scatter.73.cloned.1.call-update) | async-done | bytes 131088
  1722.4 35.2 %reduce-scatter.65.cloned.1.call-done = f32[64,1152]{1,0:T(8,128)} async-done(((f32[512,1152]{1,0:T(8,128)}), f32[64,1152]{1,0:T(8,128)}) %reduce-scatter.65.cloned.1.call-update) | async-done | bytes 294928
  1757.6 37.8 %reduce-scatter.67.cloned.1.call-done = f32[64,1152]{1,0:T(8,128)} async-done(((f32[512,1152]{1,0:T(8,128)}), f32[64,1152]{1,0:T(8,128)}) %reduce-scatter.67.cloned.1.call-update) | async-done | bytes 294928
  1795.4 37.7 %reduce-scatter.69.cloned.1.call-done = f32[64,1152]{1,0:T(8,128)} async-done(((f32[512,1152]{1,0:T(8,128)}), f32[64,1152]{1,0:T(8,128)}) %reduce-scatter.69.cloned.1.call-update) | async-done | bytes 294928
  1833.0 37.8 %reduce-scatter.71.cloned.1.call-done = f32[64,1152]{1,0:T(8,128)} async-done(((f32[512,1152]{1,0:T(8,128)}), f32[64,1152]{1,0:T(8,128)}) %reduce-scatter.71.cloned.1.call-update) | async-done | bytes 294928
  1875.8 44.7 %all-reduce.37 = (f32[1]{0:T(128)}, f32[1]{0:T(128)}, f32[]{:T(128)}, f32[8,512]{1,0:T(8,128)}) all-reduce(f32[1]{0:T(128)} %bitcast.179, f32[1]{0:T(128)} %bitcast.177, f32[]{:T(128)S(6)} %add.1351, f32[8,512]{1,0:T(8,128)} %stack.107), channel_id=1, replica_groups=mesh['dp'=8,'fsdp'=4] {'dp','fsdp'}, use_global_device_ids=true, to_apply=%region_29.32 | all-reduce | flops 4099 | bytes 32792 | tf_op jit(solution)/shard_map/psum | solution.py:322
  (1035 shorter events, 526.1 us)
Async XLA Ops:
  7.2 26.8 %all-gather.31.cloned.1.call-start = ((), (), s32[]{:S(2)}) async-start(), calls=%async_computation.34 | async-start | bytes 1327104 | tf_op jit(solution)/shard_map/all_gather | solution.py:150
  9.4 49.3 %all-gather.35.cloned.1.call-start = ((), (), s32[]{:S(2)}) async-start(), calls=%async_computation.36 | async-start | bytes 1327104 | tf_op jit(solution)/shard_map/all_gather | solution.py:150
  10.2 92.4 %all-gather.43.cloned.1.call-start = ((), (), s32[]{:S(2)}) async-start(), calls=%async_computation.40 | async-start | bytes 1327104 | tf_op jit(solution)/shard_map/all_gather | solution.py:150
  10.9 314.8 %all-gather.47.cloned.1.call-start = ((), (), s32[]{:S(2)}) async-start(), calls=%async_computation.42 | async-start | bytes 1327104 | tf_op jit(solution)/shard_map/all_gather | solution.py:150
  11.5 322.0 %all-gather.33.cloned.1.call-start = ((), (), s32[]{:S(2)}) async-start(), calls=%async_computation.35 | async-start | bytes 5898240 | tf_op jit(solution)/shard_map/all_gather | solution.py:151
  36.4 333.2 %all-gather.37.cloned.1.call-start = ((), (), s32[]{:S(2)}) async-start(), calls=%async_computation.37 | async-start | bytes 5898240 | tf_op jit(solution)/shard_map/all_gather | solution.py:151
  61.1 323.2 %all-gather.39.cloned.1.call-start = ((), (), s32[]{:S(2)}) async-start(), calls=%async_computation.38 | async-start | bytes 2621440 | tf_op jit(solution)/shard_map/all_gather | solution.py:151
  77.2 311.2 %all-gather.41.cloned.1.call-start = ((), (), s32[]{:S(2)}) async-start(), calls=%async_computation.39 | async-start | bytes 2621440 | tf_op jit(solution)/shard_map/all_gather | solution.py:151
  93.5 331.1 %all-gather.45.cloned.1.call-start = ((), (), s32[]{:S(2)}) async-start(), calls=%async_computation.41 | async-start | bytes 5898240 | tf_op jit(solution)/shard_map/all_gather | solution.py:151
  145.1 37.4 %all-to-all-start = ((s32[8,1,256]{2,1,0:T(1,128)}), s32[8,1,256]{2,1,0:T(1,128)S(1)}, u32[]{:S(2)}, u32[]{:S(2)}) async-start(s32[8,1,256]{2,1,0:T(1,128)} %reshape.3897), calls=%async_computation | async-start | bytes 16384 | tf_op jit(solution)/shard_map/all_to_all | solution.py:222
  180.4 104.8 %copy-start.8 = (f32[1024,512]{1,0:T(8,128)}, f32[1024,512]{1,0:T(8,128)S(1)}, u32[]{:S(2)}) copy-start(f32[1024,512]{1,0:T(8,128)S(1)} %fusion.236) | copy-start | bytes 6291460
  184.5 7.1 all-to-all-start.1
  201.3 56.9 %all-to-all-start.2 = ((bf16[8,4,64,256]{3,2,1,0:T(8,128)(2,1)}), bf16[8,4,64,256]{3,2,1,0:T(8,128)(2,1)}, u32[]{:S(2)}, u32[]{:S(2)}) async-start(bf16[8,4,64,256]{3,2,1,0:T(8,128)(2,1)} %broadcast_select_fusion.2), calls=%async_computation.2 | async-start | bytes 2097152 | tf_op jit(solution)/shard_map/all_to_all | solution.py:230
  253.9 66.3 %copy-start.147 = (bf16[32,32]{1,0:T(8,128)(2,1)}, bf16[32,32]{1,0:T(8,128)(2,1)S(1)}, u32[]{:S(2)}) copy-start(bf16[32,32]{1,0:T(8,128)(2,1)S(1)} %get-tuple-element.479) | copy-start | bytes 6148
  253.9 66.3 %copy-start.149 = (bf16[32,32]{1,0:T(8,128)(2,1)}, bf16[32,32]{1,0:T(8,128)(2,1)S(1)}, u32[]{:S(2)}) copy-start(bf16[32,32]{1,0:T(8,128)(2,1)S(1)} %get-tuple-element.484) | copy-start | bytes 6148
  253.9 66.3 %copy-start.151 = (bf16[32,32]{1,0:T(8,128)(2,1)}, bf16[32,32]{1,0:T(8,128)(2,1)S(1)}, u32[]{:S(2)}) copy-start(bf16[32,32]{1,0:T(8,128)(2,1)S(1)} %get-tuple-element.485) | copy-start | bytes 6148
  253.9 66.3 %copy-start.153 = (bf16[32,32]{1,0:T(8,128)(2,1)}, bf16[32,32]{1,0:T(8,128)(2,1)S(1)}, u32[]{:S(2)}) copy-start(bf16[32,32]{1,0:T(8,128)(2,1)S(1)} %get-tuple-element.488) | copy-start | bytes 6148
  260.5 65.4 %all-to-all-start.3 = ((bf16[8,4,64,256]{3,2,0,1:T(8,128)(2,1)}), bf16[8,4,64,256]{3,2,0,1:T(8,128)(2,1)}, u32[]{:S(2)}, u32[]{:S(2)}) async-start(bf16[8,4,64,256]{3,2,0,1:T(8,128)(2,1)} %copy.304), calls=%async_computation.3 | async-start | bytes 2097152 | tf_op jit(solution)/shard_map/all_to_all | solution.py:229
  266.1 184.8 %all-gather.49.cloned.1.call-start = ((), (), s32[]{:S(2)}) async-start(), calls=%async_computation.43 | async-start | bytes 5898240 | tf_op jit(solution)/shard_map/all_gather | solution.py:151
  325.8 461.3 %reduce-scatter.57.cloned.1.call-start = ((), (), s32[]{:S(2)}) async-start(), calls=%async_computation.32 | async-start | bytes 655360 | tf_op jit(solution)/shard_map/reduce_scatter | solution.py:159
  333.5 53.6 %copy-start.42 = (f32[4,256,256]{2,1,0:T(8,128)}, f32[4,256,256]{2,1,0:T(8,128)S(1)}, u32[]{:S(2)}) copy-start(f32[4,256,256]{2,1,0:T(8,128)S(1)} %fusion.175) | copy-start | bytes 3145732
  607.9 181.0 %reduce-scatter.59.cloned.1.call-start = ((), (), s32[]{:S(2)}) async-start(), calls=%async_computation.33 | async-start | bytes 655360 | tf_op jit(solution)/shard_map/reduce_scatter | solution.py:159
  639.8 150.9 %reduce-scatter.63.cloned.1.call-start = ((), (), s32[]{:S(2)}) async-start(), calls=%async_computation.45 | async-start | bytes 1966080
  658.5 134.3 %reduce-scatter.61.cloned.1.call-start = ((), (), s32[]{:S(2)}) async-start(), calls=%async_computation.44 | async-start | bytes 1966080
  707.0 138.6 %reduce-scatter.55.cloned.1.call-start = ((), (), s32[]{:S(2)}) async-start(), calls=%async_computation.31 | async-start | bytes 5242880 | tf_op jit(solution)/shard_map/reduce_scatter | solution.py:159
  709.9 139.1 %reduce-scatter.53.cloned.1.call-start = ((), (), s32[]{:S(2)}) async-start(), calls=%async_computation.30 | async-start | bytes 5242880 | tf_op jit(solution)/shard_map/reduce_scatter | solution.py:159
  714.1 233.0 %reduce-scatter.45.cloned.1.call-start = ((), (), s32[]{:S(2)}) async-start(), calls=%async_computation.26 | async-start | bytes 11796480 | tf_op jit(solution)/shard_map/reduce_scatter | solution.py:159
  730.8 314.3 %reduce-scatter.47.cloned.1.call-start = ((), (), s32[]{:S(2)}) async-start(), calls=%async_computation.27 | async-start | bytes 11796480 | tf_op jit(solution)/shard_map/reduce_scatter | solution.py:159
  748.0 395.2 %reduce-scatter.49.cloned.1.call-start = ((), (), s32[]{:S(2)}) async-start(), calls=%async_computation.28 | async-start | bytes 11796480 | tf_op jit(solution)/shard_map/reduce_scatter | solution.py:159
  769.9 471.4 %reduce-scatter.51.cloned.1.call-start = ((), (), s32[]{:S(2)}) async-start(), calls=%async_computation.29 | async-start | bytes 11796480 | tf_op jit(solution)/shard_map/reduce_scatter | solution.py:159
  787.0 483.9 %reduce-scatter.77.cloned.1.call-start = ((), (), s32[]{:S(2)}) async-start(), calls=%async_computation.52 | async-start | bytes 147456
  788.8 513.2 %reduce-scatter.79.cloned.1.call-start = ((), (), s32[]{:S(2)}) async-start(), calls=%async_computation.53 | async-start | bytes 147456
  790.6 543.4 %reduce-scatter.43.cloned.1.call-start = ((), (), s32[]{:S(2)}) async-start(), calls=%async_computation.25 | async-start | bytes 589824 | tf_op jit(solution)/shard_map/reduce_scatter | solution.py:160
  792.7 573.2 %reduce-scatter.41.cloned.1.call-start = ((), (), s32[]{:S(2)}) async-start(), calls=%async_computation.24 | async-start | bytes 589824 | tf_op jit(solution)/shard_map/reduce_scatter | solution.py:160
  794.8 861.0 %all-reduce.41.cloned.1.call-start = ((), (), s32[]{:S(2)}) async-start(), calls=%async_computation.54 | async-start | bytes 33685504 | tf_op jit(solution)/shard_map/psum | solution.py:358
  845.6 841.6 %reduce-scatter.75.cloned.1.call-start = ((), (), s32[]{:S(2)}) async-start(), calls=%async_computation.51 | async-start | bytes 1179648
  848.2 872.5 %reduce-scatter.73.cloned.1.call-start = ((), (), s32[]{:S(2)}) async-start(), calls=%async_computation.50 | async-start | bytes 1179648
  851.6 905.9 %reduce-scatter.65.cloned.1.call-start = ((), (), s32[]{:S(2)}) async-start(), calls=%async_computation.46 | async-start | bytes 2654208
  950.1 845.2 %reduce-scatter.67.cloned.1.call-start = ((), (), s32[]{:S(2)}) async-start(), calls=%async_computation.47 | async-start | bytes 2654208
  1048.2 784.8 %reduce-scatter.69.cloned.1.call-start = ((), (), s32[]{:S(2)}) async-start(), calls=%async_computation.48 | async-start | bytes 2654208
  1146.4 724.5 %reduce-scatter.71.cloned.1.call-start = ((), (), s32[]{:S(2)}) async-start(), calls=%async_computation.49 | async-start | bytes 2654208
  1244.5 411.4 %copy-start.207 = (f32[512]{0:T(512)S(1)}, f32[512]{0:T(512)}, u32[]{:S(2)}) copy-start(f32[512]{0:T(512)} %param.48) | copy-start | bytes 6148
  1244.5 412.1 %copy-start.120 = (f32[512,256]{1,0:T(8,128)S(1)}, f32[512,256]{1,0:T(8,128)}, u32[]{:S(2)}) copy-start(f32[512,256]{1,0:T(8,128)} %param.49) | copy-start | bytes 1572868
  1302.9 568.0 %copy-start.163 = (f32[1,128,32]{1,2,0:T(8,128)}, f32[1,128,32]{1,2,0:T(8,128)S(1)}, u32[]{:S(2)}) copy-start(f32[1,128,32]{1,2,0:T(8,128)S(1)} %copy.328) | copy-start | bytes 49156
  1656.6 214.3 %copy-start.208 = (f32[512]{0:T(512)}, f32[512]{0:T(512)S(1)}, u32[]{:S(2)}) copy-start(f32[512]{0:T(512)S(1)} %multiply_add_fusion.10) | copy-start | bytes 6148
  1870.9 59.5 %copy-start.46 = (f32[4,1152,64]{1,2,0:T(8,128)S(1)}, f32[4,1152,64]{1,2,0:T(8,128)}, u32[]{:S(2)}) copy-start(f32[4,1152,64]{1,2,0:T(8,128)} %param.34) | copy-start | bytes 3538948
  1870.9 59.5 %copy-start.125 = (f32[4,1152,64]{1,2,0:T(8,128)S(1)}, f32[4,1152,64]{1,2,0:T(8,128)}, u32[]{:S(2)}) copy-start(f32[4,1152,64]{1,2,0:T(8,128)} %param.39) | copy-start | bytes 3538948
  1870.9 59.5 %copy-start.126 = (f32[4,1152,64]{1,2,0:T(8,128)S(1)}, f32[4,1152,64]{1,2,0:T(8,128)}, u32[]{:S(2)}) copy-start(f32[4,1152,64]{1,2,0:T(8,128)} %param.44) | copy-start | bytes 3538948
  (212 other events, 857.9 us)
Sparse Core Ops, SparseCore 0:
  10.2 23.7 all-gather.30
  36.2 22.4 all-gather.34
  60.9 23.7 all-gather.42
  86.8 22.9 all-gather.46
  112.1 56.5 all-gather.32
  171.0 57.1 all-gather.36
  230.0 35.1 all-gather.38
  267.0 40.4 all-gather.40
  310.0 57.5 all-gather.44
  369.3 57.0 all-gather.48
  608.0 24.4 reduce-scatter.56
  639.9 24.4 reduce-scatter.58
  667.4 30.8 reduce-scatter.62
  707.1 30.5 reduce-scatter.60
  740.6 52.6 reduce-scatter.54
  796.3 52.6 reduce-scatter.52
  852.0 94.9 reduce-scatter.44
  950.0 95.0 reduce-scatter.46
  1048.2 95.0 reduce-scatter.48
  1146.2 95.0 reduce-scatter.50
  1244.1 26.7 reduce-scatter.76
  1273.8 28.2 reduce-scatter.78
  1304.9 29.0 reduce-scatter.42
  1336.8 29.0 reduce-scatter.40
  1372.9 282.9 all-reduce.40
  1658.6 28.5 reduce-scatter.74
  1689.9 30.8 reduce-scatter.72
  1723.1 34.4 reduce-scatter.64
  1759.9 35.4 reduce-scatter.66
  1797.5 35.4 reduce-scatter.68
  1835.4 35.4 reduce-scatter.70
where the time goes:
time: 1960 us; the launch traced here: 1940 us
  waiting for transfers between devices  1050 us (54%)
  matrix products  256 us (13%)
  blocking collectives  237 us (12%)
  local copies, waits for them, and re-layouts  188 us (10%)
  other arithmetic  170 us (9%)
  between operations  24.2 us (1%)
  starting transfers between devices  22.2 us (1%)
    reduce_scatter x8, waiting for transfers between devices, reduce_grad(): rows = lax.psum_scatter(full, 'fsdp', scatter_dimension=0, tiled=True)  381 us
    psum x1, waiting for transfers between devices, on_device(): sums_total, counts_total = lax.psum((sums_all, counts_all), ('dp', 'fsdp'))  288 us
    unnamed x41, waiting for transfers between devices  268 us
    all_gather x6, blocking collectives, fetch(): cols = lax.all_gather(shard.astype(jnp.bfloat16), 'dp', axis=1, tiled=True)  106 us
    dot_general x49, matrix products, along_rows(): lax.dot_general(left, right, (((0,), (0,)), ((), ())), preferred_element_...  103 us
    dot_general x41, matrix products, along_cols(): lax.dot_general(left, right, (((1,), (1,)), ((), ())), preferred_element_...  88.1 us
    reduce_scatter x2, waiting for transfers between devices, reduce_grad(): return lax.psum_scatter(rows, 'dp', scatter_dimension=1, tiled=True)  62.3 us
    unnamed x467, local copies, waits for them, and re-layouts  60.6 us
  transfers between devices with their start and end apart: 35, of which 19 were waited for; matrix products, arithmetic and copies ran while one was open for 24% of the time, Pallas kernels for 0%

commit v1 on v0

--- a/solution.py
+++ b/solution.py
@@ -355,7 +355,9 @@
     sums_all, counts_all = lax.map(code_block, jnp.arange(0, K, block_len, dtype=jnp.int32))
     sums_all = sums_all.reshape(K, ZD)
     counts_all = counts_all.reshape(K)
-    sums_total, counts_total = lax.psum((sums_all, counts_all), ("dp", "fsdp"))
+    sums_total, counts_total = lax.psum(
+        lax.psum((sums_all, counts_all), axis_name="fsdp"), axis_name="dp"
+    )
     start_row = lax.axis_index(("dp", "fsdp")) * rows
     my_sums = lax.dynamic_slice_in_dim(sums_total, start_row, rows, 0)
     my_counts = lax.dynamic_slice_in_dim(counts_total, start_row, rows, 0)

time: 1960 us -> 2260 us (1.15)
  waiting for transfers between devices: 1050 us -> 1350 us
    psum x1 -> x2, waiting for transfers between devices: 288 us -> 585 us  [the longest x1 310 us: on_device(): lax.psum((sums_all, counts_all), axis_name='fsdp')]
    unnamed x41 -> x42, waiting for transfers between devices: 268 us -> 275 us
    unnamed x467 -> x471, local copies, waits for them, and re-layouts: 60.6 us -> 61.4 us
  transfers between devices with their start and end apart: 35 -> 36, of which waited for: 19 -> 20; matrix products, arithmetic and copies ran while one was open for 24% -> 21% of each run, Pallas kernels for 0% -> 0%
where the time goes in v1:
time: 2260 us; the launch traced here: 2250 us
  waiting for transfers between devices  1350 us (60%)
  matrix products  256 us (11%)
  blocking collectives  238 us (11%)
  local copies, waits for them, and re-layouts  189 us (8%)
  other arithmetic  170 us (8%)
  between operations  23.9 us (1%)
    reduce_scatter x8, waiting for transfers between devices, reduce_grad(): rows = lax.psum_scatter(full, 'fsdp', scatter_dimension=0, tiled=True)  380 us
    psum x1, waiting for transfers between devices, on_device(): lax.psum((sums_all, counts_all), axis_name='fsdp')  310 us
    unnamed x42, waiting for transfers between devices  275 us
    psum x1, waiting for transfers between devices, on_device(): lax.psum(lax.psum((sums_all, counts_all), axis_name='fsdp'), axis_name='dp')  275 us
    all_gather x6, blocking collectives, fetch(): cols = lax.all_gather(shard.astype(jnp.bfloat16), 'dp', axis=1, tiled=True)  105 us
    dot_general x49, matrix products, along_rows(): lax.dot_general(left, right, (((0,), (0,)), ((), ())), preferred_element_...  103 us
    dot_general x41, matrix products, along_cols(): lax.dot_general(left, right, (((1,), (1,)), ((), ())), preferred_element_...  87.8 us
    reduce_scatter x2, waiting for transfers between devices, reduce_grad(): return lax.psum_scatter(rows, 'dp', scatter_dimension=1, tiled=True)  62.3 us
  transfers between devices with their start and end apart: 36, of which 20 were waited for; matrix products, arithmetic and copies ran while one was open for 21% of the time, Pallas kernels for 0%

profile of v1, /device:TPU:12, one launch (start us, length us, event | category | flops | bytes accessed | tf_op | source)
XLA Modules:
  0.0 2249.8 jit_solution(12234728035799786868)
XLA Ops:
  11.5 22.5 all-gather.31.cloned.1.call-done
  36.5 22.2 all-gather.35.cloned.1.call-done
  61.2 15.9 all-gather.6
  77.2 16.3 all-gather.12
  105.0 8.0 while.37
  119.2 15.8 fusion.437
  145.0 5.2 all-to-all-start
  150.9 14.2 all-gather
  165.3 12.4 all-gather.1
  192.4 7.5 gather_fusion.2
  201.2 5.2 all-to-all-start.2
  208.3 29.5 %all-gather.10 = bf16[1,128,256]{1,2,0:T(8,128)(2,1)S(1)} all-gather(bf16[1,128,32]{1,2,0:T(8,128)(2,1)S(1)} %get-tuple-element.457), channel_id=12, replica_groups=mesh['dp'=8,'fsdp'=4] {'dp'}, dimensions={2}, use_global_device_ids=true | all-gather | bytes 73728 | tf_op jit(solution)/shard_map/all_gather | solution.py:150
  237.9 14.3 all-gather.18
  260.3 5.8 all-to-all-start.3
  266.1 15.2 all-gather.8
  287.6 11.5 all-gather.9
  299.1 9.0 all-gather.11
  308.1 12.0 all-gather.19
  320.1 5.4 fusion.150
  364.0 5.3 fusion.158
  419.2 5.2 fusion.166
  445.3 5.4 fusion.174
  464.6 6.5 multiply_reduce_fusion
  471.2 41.7 %psum.64 = f32[]{:T(128)} all-reduce(f32[]{:T(128)} %get-tuple-element.298), channel_id=1, replica_groups=mesh['dp'=8,'fsdp'=4] {'dp','fsdp'}, use_global_device_ids=true, to_apply=%region_27.30 | all-reduce | flops 1 | bytes 8 | tf_op jit(solution)/shard_map/psum | solution.py:217
  512.9 6.2 divide_convert_fusion
  565.6 9.8 fusion.495
  579.9 5.7 fusion.511
  627.8 7.9 fusion.496
  641.4 5.3 fusion.510
  671.7 8.5 fusion.497
  787.9 49.7 %while.36 = (s32[]{:T(128)}, f32[8,2048,256]{2,1,0:T(8,128)}, f32[8,2048]{1,0:T(8,128)S(1)}, s32[4,256]{1,0:T(4,128)S(1)}, s32[8]{0:T(128)S(1)}, /*index=5*/bf16[1024,256]{1,0:T(8,128)(2,1)S(1)}, s32[]{:T(128)}, s32[]{:T(128)}) while((s32[]{:T(128)}, f32[8,2048,256]{2,1,0:T(8,128)}, f32[8,2048]{1,0:T(8,128)S(1)}, s32[4,256]{1,0:T(4,128)S(1)}, ...), condition=%wide.region_84.87_spmd, body=%wide.region_82.86_spmd.sunk | while | flops 1084227584 | bytes 2687093 | solution.py:355
  851.6 95.4 %reduce-scatter.45.cloned.1.call-done = f32[1152,512]{1,0:T(8,128)} async-done(((f32[4608,512]{1,0:T(8,128)}), f32[1152,512]{1,0:T(8,128)}) %reduce-scatter.45.cloned.1.call-update) | async-done | bytes 2359312 | tf_op jit(solution)/shard_map/reduce_scatter | solution.py:159
  950.1 94.9 %reduce-scatter.47.cloned.1.call-done = f32[1152,512]{1,0:T(8,128)} async-done(((f32[4608,512]{1,0:T(8,128)}), f32[1152,512]{1,0:T(8,128)}) %reduce-scatter.47.cloned.1.call-update) | async-done | bytes 2359312 | tf_op jit(solution)/shard_map/reduce_scatter | solution.py:159
  1048.2 95.0 %reduce-scatter.49.cloned.1.call-done = f32[1152,512]{1,0:T(8,128)} async-done(((f32[4608,512]{1,0:T(8,128)}), f32[1152,512]{1,0:T(8,128)}) %reduce-scatter.49.cloned.1.call-update) | async-done | bytes 2359312 | tf_op jit(solution)/shard_map/reduce_scatter | solution.py:159
  1146.3 94.9 %reduce-scatter.51.cloned.1.call-done = f32[1152,512]{1,0:T(8,128)} async-done(((f32[4608,512]{1,0:T(8,128)}), f32[1152,512]{1,0:T(8,128)}) %reduce-scatter.51.cloned.1.call-update) | async-done | bytes 2359312 | tf_op jit(solution)/shard_map/reduce_scatter | solution.py:159
  1244.4 310.0 %all-reduce.45.cloned.1.call-done = (f32[16384]{0:T(1024)}, f32[16384,256]{1,0:T(8,128)}) async-done(((f32[16384]{0:T(1024)}, f32[16384,256]{1,0:T(8,128)}), (f32[16384]{0:T(1024)}, f32[16384,256]{1,0:T(8,128)})) %all-reduce.45.cloned.1.call-update) | async-done | bytes 16842768 | tf_op jit(solution)/shard_map/psum | solution.py:359
  1555.8 28.7 %reduce-scatter.77.cloned.1.call-done = f32[32,128]{1,0:T(8,128)} async-done(((f32[256,128]{1,0:T(8,128)}), f32[32,128]{1,0:T(8,128)}) %reduce-scatter.77.cloned.1.call-update) | async-done | bytes 16400
  1585.4 30.2 %reduce-scatter.79.cloned.1.call-done = f32[32,128]{1,0:T(8,128)} async-done(((f32[256,128]{1,0:T(8,128)}), f32[32,128]{1,0:T(8,128)}) %reduce-scatter.79.cloned.1.call-update) | async-done | bytes 16400
  1617.1 30.4 %reduce-scatter.43.cloned.1.call-done = f32[192,64]{0,1:T(8,128)} async-done(((f32[192,512]{0,1:T(8,128)}), f32[192,64]{0,1:T(8,128)}) %reduce-scatter.43.cloned.1.call-update) | async-done | bytes 49168 | tf_op jit(solution)/shard_map/reduce_scatter | solution.py:160
  1647.5 31.9 %reduce-scatter.41.cloned.1.call-done = f32[192,64]{0,1:T(8,128)} async-done(((f32[192,512]{0,1:T(8,128)}), f32[192,64]{0,1:T(8,128)}) %reduce-scatter.41.cloned.1.call-update) | async-done | bytes 49168 | tf_op jit(solution)/shard_map/reduce_scatter | solution.py:160
  1680.9 31.8 %reduce-scatter.75.cloned.1.call-done = f32[64,512]{1,0:T(8,128)} async-done(((f32[512,512]{1,0:T(8,128)}), f32[64,512]{1,0:T(8,128)}) %reduce-scatter.75.cloned.1.call-update) | async-done | bytes 131088
  1712.7 33.1 %reduce-scatter.73.cloned.1.call-done = f32[64,512]{1,0:T(8,128)} async-done(((f32[512,512]{1,0:T(8,128)}), f32[64,512]{1,0:T(8,128)}) %reduce-scatter.73.cloned.1.call-update) | async-done | bytes 131088
  1747.5 35.6 %reduce-scatter.65.cloned.1.call-done = f32[64,1152]{1,0:T(8,128)} async-done(((f32[512,1152]{1,0:T(8,128)}), f32[64,1152]{1,0:T(8,128)}) %reduce-scatter.65.cloned.1.call-update) | async-done | bytes 294928
  1783.0 37.9 %reduce-scatter.67.cloned.1.call-done = f32[64,1152]{1,0:T(8,128)} async-done(((f32[512,1152]{1,0:T(8,128)}), f32[64,1152]{1,0:T(8,128)}) %reduce-scatter.67.cloned.1.call-update) | async-done | bytes 294928
  1820.9 37.8 %reduce-scatter.69.cloned.1.call-done = f32[64,1152]{1,0:T(8,128)} async-done(((f32[512,1152]{1,0:T(8,128)}), f32[64,1152]{1,0:T(8,128)}) %reduce-scatter.69.cloned.1.call-update) | async-done | bytes 294928
  1858.7 37.9 %reduce-scatter.71.cloned.1.call-done = f32[64,1152]{1,0:T(8,128)} async-done(((f32[512,1152]{1,0:T(8,128)}), f32[64,1152]{1,0:T(8,128)}) %reduce-scatter.71.cloned.1.call-update) | async-done | bytes 294928
  1901.5 46.2 %all-reduce.37 = (f32[1]{0:T(128)}, f32[1]{0:T(128)}, f32[]{:T(128)}, f32[8,512]{1,0:T(8,128)}) all-reduce(f32[1]{0:T(128)} %bitcast.179, f32[1]{0:T(128)} %bitcast.177, f32[]{:T(128)S(6)} %add.1355, f32[8,512]{1,0:T(8,128)} %stack.107), channel_id=1, replica_groups=mesh['dp'=8,'fsdp'=4] {'dp','fsdp'}, use_global_device_ids=true, to_apply=%region_29.32 | all-reduce | flops 4099 | bytes 32792 | tf_op jit(solution)/shard_map/psum | solution.py:322
  1964.0 274.7 %all-reduce.43.cloned.1.call-done = (f32[16384]{0:T(1024)}, f32[16384,256]{1,0:T(8,128)}) async-done(((f32[16384]{0:T(1024)}, f32[16384,256]{1,0:T(8,128)}), (f32[16384]{0:T(1024)}, f32[16384,256]{1,0:T(8,128)})) %all-reduce.43.cloned.1.call-update) | async-done | bytes 16842768 | tf_op jit(solution)/shard_map/psum | solution.py:358
  (1042 shorter events, 531.5 us)
Async XLA Ops:
  7.2 26.8 %all-gather.31.cloned.1.call-start = ((), (), s32[]{:S(2)}) async-start(), calls=%async_computation.34 | async-start | bytes 1327104 | tf_op jit(solution)/shard_map/all_gather | solution.py:150
  9.4 49.3 %all-gather.35.cloned.1.call-start = ((), (), s32[]{:S(2)}) async-start(), calls=%async_computation.36 | async-start | bytes 1327104 | tf_op jit(solution)/shard_map/all_gather | solution.py:150
  10.2 92.4 %all-gather.43.cloned.1.call-start = ((), (), s32[]{:S(2)}) async-start(), calls=%async_computation.40 | async-start | bytes 1327104 | tf_op jit(solution)/shard_map/all_gather | solution.py:150
  10.9 314.6 %all-gather.47.cloned.1.call-start = ((), (), s32[]{:S(2)}) async-start(), calls=%async_computation.42 | async-start | bytes 1327104 | tf_op jit(solution)/shard_map/all_gather | solution.py:150
  11.5 321.9 %all-gather.33.cloned.1.call-start = ((), (), s32[]{:S(2)}) async-start(), calls=%async_computation.35 | async-start | bytes 5898240 | tf_op jit(solution)/shard_map/all_gather | solution.py:151
  36.4 332.9 %all-gather.37.cloned.1.call-start = ((), (), s32[]{:S(2)}) async-start(), calls=%async_computation.37 | async-start | bytes 5898240 | tf_op jit(solution)/shard_map/all_gather | solution.py:151
  61.1 323.0 %all-gather.39.cloned.1.call-start = ((), (), s32[]{:S(2)}) async-start(), calls=%async_computation.38 | async-start | bytes 2621440 | tf_op jit(solution)/shard_map/all_gather | solution.py:151
  77.2 311.0 %all-gather.41.cloned.1.call-start = ((), (), s32[]{:S(2)}) async-start(), calls=%async_computation.39 | async-start | bytes 2621440 | tf_op jit(solution)/shard_map/all_gather | solution.py:151
  93.5 330.9 %all-gather.45.cloned.1.call-start = ((), (), s32[]{:S(2)}) async-start(), calls=%async_computation.41 | async-start | bytes 5898240 | tf_op jit(solution)/shard_map/all_gather | solution.py:151
  145.0 37.4 %all-to-all-start = ((s32[8,1,256]{2,1,0:T(1,128)}), s32[8,1,256]{2,1,0:T(1,128)S(1)}, u32[]{:S(2)}, u32[]{:S(2)}) async-start(s32[8,1,256]{2,1,0:T(1,128)} %reshape.3897), calls=%async_computation | async-start | bytes 16384 | tf_op jit(solution)/shard_map/all_to_all | solution.py:222
  180.3 104.8 %copy-start.8 = (f32[1024,512]{1,0:T(8,128)}, f32[1024,512]{1,0:T(8,128)S(1)}, u32[]{:S(2)}) copy-start(f32[1024,512]{1,0:T(8,128)S(1)} %fusion.236) | copy-start | bytes 6291460
  184.4 7.1 all-to-all-start.1
  201.2 56.8 %all-to-all-start.2 = ((bf16[8,4,64,256]{3,2,1,0:T(8,128)(2,1)}), bf16[8,4,64,256]{3,2,1,0:T(8,128)(2,1)}, u32[]{:S(2)}, u32[]{:S(2)}) async-start(bf16[8,4,64,256]{3,2,1,0:T(8,128)(2,1)} %broadcast_select_fusion.2), calls=%async_computation.2 | async-start | bytes 2097152 | tf_op jit(solution)/shard_map/all_to_all | solution.py:230
  253.8 66.3 %copy-start.148 = (bf16[32,32]{1,0:T(8,128)(2,1)}, bf16[32,32]{1,0:T(8,128)(2,1)S(1)}, u32[]{:S(2)}) copy-start(bf16[32,32]{1,0:T(8,128)(2,1)S(1)} %get-tuple-element.481) | copy-start | bytes 6148
  253.8 66.3 %copy-start.150 = (bf16[32,32]{1,0:T(8,128)(2,1)}, bf16[32,32]{1,0:T(8,128)(2,1)S(1)}, u32[]{:S(2)}) copy-start(bf16[32,32]{1,0:T(8,128)(2,1)S(1)} %get-tuple-element.486) | copy-start | bytes 6148
  253.8 66.3 %copy-start.152 = (bf16[32,32]{1,0:T(8,128)(2,1)}, bf16[32,32]{1,0:T(8,128)(2,1)S(1)}, u32[]{:S(2)}) copy-start(bf16[32,32]{1,0:T(8,128)(2,1)S(1)} %get-tuple-element.487) | copy-start | bytes 6148
  253.8 66.3 %copy-start.154 = (bf16[32,32]{1,0:T(8,128)(2,1)}, bf16[32,32]{1,0:T(8,128)(2,1)S(1)}, u32[]{:S(2)}) copy-start(bf16[32,32]{1,0:T(8,128)(2,1)S(1)} %get-tuple-element.490) | copy-start | bytes 6148
  260.3 65.3 %all-to-all-start.3 = ((bf16[8,4,64,256]{3,2,0,1:T(8,128)(2,1)}), bf16[8,4,64,256]{3,2,0,1:T(8,128)(2,1)}, u32[]{:S(2)}, u32[]{:S(2)}) async-start(bf16[8,4,64,256]{3,2,0,1:T(8,128)(2,1)} %copy.304), calls=%async_computation.3 | async-start | bytes 2097152 | tf_op jit(solution)/shard_map/all_to_all | solution.py:229
  266.1 184.6 %all-gather.49.cloned.1.call-start = ((), (), s32[]{:S(2)}) async-start(), calls=%async_computation.43 | async-start | bytes 5898240 | tf_op jit(solution)/shard_map/all_gather | solution.py:151
  325.6 512.8 %reduce-scatter.57.cloned.1.call-start = ((), (), s32[]{:S(2)}) async-start(), calls=%async_computation.32 | async-start | bytes 655360 | tf_op jit(solution)/shard_map/reduce_scatter | solution.py:159
  607.9 232.2 %reduce-scatter.59.cloned.1.call-start = ((), (), s32[]{:S(2)}) async-start(), calls=%async_computation.33 | async-start | bytes 655360 | tf_op jit(solution)/shard_map/reduce_scatter | solution.py:159
  639.7 202.2 %reduce-scatter.63.cloned.1.call-start = ((), (), s32[]{:S(2)}) async-start(), calls=%async_computation.45 | async-start | bytes 1966080
  658.4 185.5 %reduce-scatter.61.cloned.1.call-start = ((), (), s32[]{:S(2)}) async-start(), calls=%async_computation.44 | async-start | bytes 1966080
  706.9 139.2 %reduce-scatter.55.cloned.1.call-start = ((), (), s32[]{:S(2)}) async-start(), calls=%async_computation.31 | async-start | bytes 5242880 | tf_op jit(solution)/shard_map/reduce_scatter | solution.py:159
  709.8 139.2 %reduce-scatter.53.cloned.1.call-start = ((), (), s32[]{:S(2)}) async-start(), calls=%async_computation.30 | async-start | bytes 5242880 | tf_op jit(solution)/shard_map/reduce_scatter | solution.py:159
  713.9 233.1 %reduce-scatter.45.cloned.1.call-start = ((), (), s32[]{:S(2)}) async-start(), calls=%async_computation.26 | async-start | bytes 11796480 | tf_op jit(solution)/shard_map/reduce_scatter | solution.py:159
  730.7 314.3 %reduce-scatter.47.cloned.1.call-start = ((), (), s32[]{:S(2)}) async-start(), calls=%async_computation.27 | async-start | bytes 11796480 | tf_op jit(solution)/shard_map/reduce_scatter | solution.py:159
  747.9 395.3 %reduce-scatter.49.cloned.1.call-start = ((), (), s32[]{:S(2)}) async-start(), calls=%async_computation.28 | async-start | bytes 11796480 | tf_op jit(solution)/shard_map/reduce_scatter | solution.py:159
  769.7 471.5 %reduce-scatter.51.cloned.1.call-start = ((), (), s32[]{:S(2)}) async-start(), calls=%async_computation.29 | async-start | bytes 11796480 | tf_op jit(solution)/shard_map/reduce_scatter | solution.py:159
  786.9 767.4 %all-reduce.45.cloned.1.call-start = ((), (), s32[]{:S(2)}) async-start(), calls=%async_computation.55 | async-start | bytes 33685504 | tf_op jit(solution)/shard_map/psum | solution.py:359
  838.3 746.2 %reduce-scatter.77.cloned.1.call-start = ((), (), s32[]{:S(2)}) async-start(), calls=%async_computation.52 | async-start | bytes 147456
  840.1 775.5 %reduce-scatter.79.cloned.1.call-start = ((), (), s32[]{:S(2)}) async-start(), calls=%async_computation.53 | async-start | bytes 147456
  841.8 805.7 %reduce-scatter.43.cloned.1.call-start = ((), (), s32[]{:S(2)}) async-start(), calls=%async_computation.25 | async-start | bytes 589824 | tf_op jit(solution)/shard_map/reduce_scatter | solution.py:160
  843.9 835.5 %reduce-scatter.41.cloned.1.call-start = ((), (), s32[]{:S(2)}) async-start(), calls=%async_computation.24 | async-start | bytes 589824 | tf_op jit(solution)/shard_map/reduce_scatter | solution.py:160
  846.0 866.7 %reduce-scatter.75.cloned.1.call-start = ((), (), s32[]{:S(2)}) async-start(), calls=%async_computation.51 | async-start | bytes 1179648
  848.7 897.2 %reduce-scatter.73.cloned.1.call-start = ((), (), s32[]{:S(2)}) async-start(), calls=%async_computation.50 | async-start | bytes 1179648
  851.5 931.5 %reduce-scatter.65.cloned.1.call-start = ((), (), s32[]{:S(2)}) async-start(), calls=%async_computation.46 | async-start | bytes 2654208
  950.1 870.8 %reduce-scatter.67.cloned.1.call-start = ((), (), s32[]{:S(2)}) async-start(), calls=%async_computation.47 | async-start | bytes 2654208
  1048.1 810.5 %reduce-scatter.69.cloned.1.call-start = ((), (), s32[]{:S(2)}) async-start(), calls=%async_computation.48 | async-start | bytes 2654208
  1146.3 750.3 %reduce-scatter.71.cloned.1.call-start = ((), (), s32[]{:S(2)}) async-start(), calls=%async_computation.49 | async-start | bytes 2654208
  1244.3 994.4 %all-reduce.43.cloned.1.call-start = ((), (), s32[]{:S(2)}) async-start(), calls=%async_computation.54 | async-start | bytes 33685504 | tf_op jit(solution)/shard_map/psum | solution.py:358
  1554.4 398.5 %copy-start.187 = (f32[8,512]{1,0:T(8,128)S(1)}, f32[8,512]{1,0:T(8,128)}, u32[]{:S(2)}) copy-start(f32[8,512]{1,0:T(8,128)} %param.37) | copy-start | bytes 49156
  1554.4 399.9 %copy-start.165 = (f32[2,128,32]{1,2,0:T(8,128)S(1)}, f32[2,128,32]{1,2,0:T(8,128)}, u32[]{:S(2)}) copy-start(f32[2,128,32]{1,2,0:T(8,128)} %param.36) | copy-start | bytes 98308
  1554.4 401.3 %copy-start.138 = (f32[2,192,64]{1,2,0:T(8,128)S(1)}, f32[2,192,64]{1,2,0:T(8,128)}, u32[]{:S(2)}) copy-start(f32[2,192,64]{1,2,0:T(8,128)} %param.33) | copy-start | bytes 294916
  1554.5 403.1 %copy-start.131 = (f32[2,512,64]{1,2,0:T(8,128)S(1)}, f32[2,512,64]{1,2,0:T(8,128)}, u32[]{:S(2)}) copy-start(f32[2,512,64]{1,2,0:T(8,128)} %param.35) | copy-start | bytes 786436
  1712.7 244.9 %copy-start.139 = (f32[64,512]{1,0:T(8,128)S(1)}, f32[64,512]{1,0:T(8,128)}, u32[]{:S(2)}) copy-start(f32[64,512]{1,0:T(8,128)} %reduce-scatter.75.cloned.1.call-done) | copy-start | bytes 393220
  1959.8 279.0 %copy-start.209 = (f32[512]{0:T(512)S(1)}, f32[512]{0:T(512)}, u32[]{:S(2)}) copy-start(f32[512]{0:T(512)} %param.48) | copy-start | bytes 6148
  1959.8 279.7 %copy-start.120 = (f32[512,256]{1,0:T(8,128)S(1)}, f32[512,256]{1,0:T(8,128)}, u32[]{:S(2)}) copy-start(f32[512,256]{1,0:T(8,128)} %param.49) | copy-start | bytes 1572868
  (215 other events, 1130.3 us)
Sparse Core Ops, SparseCore 0:
  10.2 23.7 all-gather.30
  36.2 22.4 all-gather.34
  60.9 23.7 all-gather.42
  86.8 22.9 all-gather.46
  112.1 56.5 all-gather.32
  171.0 57.2 all-gather.36
  230.1 35.1 all-gather.38
  267.1 40.3 all-gather.40
  309.9 57.5 all-gather.44
  369.2 57.0 all-gather.48
  608.0 24.4 reduce-scatter.56
  639.9 24.4 reduce-scatter.58
  667.3 30.9 reduce-scatter.62
  707.0 30.6 reduce-scatter.60
  740.5 52.6 reduce-scatter.54
  796.3 52.6 reduce-scatter.52
  851.9 95.0 reduce-scatter.44
  950.0 95.0 reduce-scatter.46
  1048.1 95.0 reduce-scatter.48
  1146.1 95.0 reduce-scatter.50
  1245.5 308.8 all-reduce.44
  1557.2 27.2 reduce-scatter.76
  1587.3 28.2 reduce-scatter.78
  1618.4 29.0 reduce-scatter.42
  1650.3 29.0 reduce-scatter.40
  1682.2 30.4 reduce-scatter.74
  1715.5 30.2 reduce-scatter.72
  1748.2 34.7 reduce-scatter.64
  1785.5 35.3 reduce-scatter.66
  1823.2 35.4 reduce-scatter.68
  1861.1 35.4 reduce-scatter.70
  1899.4 339.2 all-reduce.42
